TPU v7x, 256 devices: a whole 4x4x8 slice. The times are simulated.
256 devices in a mesh: head: 4 (over x), seq: 64 (over z, y, core).
Axes of the slice: x: 4, y: 4, z: 8, core: 2. Of those that a mesh axis runs over, the one named last changes fastest.
Arguments:
- queries: bfloat16 [16384, 3072], P(('head', 'seq')), may hold values from -6 to 6
- key_rows: bfloat16 [49152, 3072], P('seq', 'head'), may hold values from -6 to 6
- values: bfloat16 [49152, 3072], P('seq', 'head'), may hold values from -6 to 6
- w_out: bfloat16 [3072, 6144], P('head'), may hold values from -1.1953125 to 1.1953125
- picked: int32 [256, 24], replicated, may hold values from 0 to 767, as said below
- counts: int32 [256], replicated, may hold values from 8 to 24
- tile_home: int32 [768], replicated, may hold values from 0 to 767, as said below
Outputs:
- layer_out: bfloat16 [16384, 6144], P(('head', 'seq'))
Inputs may be any that keep to these rules, and one draw needn't show every extreme that they name: `picked`: query tiles j with the same j modulo the number of devices along seq form a group. The used entries of one group are distinct key tiles; key tile t is stored on owner tile_home[t] // 12, and at most 2 used entries of one group are stored on one owner, exactly 2 for some owner in every group. `tile_home`: A permutation of the key tiles.
All inputs are finite; a program needn't handle non-finite values.
Results may differ from a plain program's by a relative error of at most 0.009.
Values may be sent and summed in bfloat16 or wider, within the bound.
No kernel may reach another device: no remote copies, remote signals or barrier semaphores. Data moves between devices by JAX's collectives and lax.ppermute only.
A program may use at most 128 MiB of HBM per device.

v0:
```python
import jax
import jax.numpy as jnp
from jax import lax
from jax.sharding import PartitionSpec as P

HD = 128
MAXSEL = 24


def body(queries, key_rows, values, w_out, picked, counts, tile_home):
    head_count = lax.axis_size("head")
    seq_count = lax.axis_size("seq")
    seq_index = lax.axis_index("seq")
    tile_rows = queries.shape[0]
    width_local = w_out.shape[0]
    heads_local = width_local // HD
    tiles_dev = key_rows.shape[0] // tile_rows
    capacity = max(2, head_count * MAXSEL // seq_count)
    request_count = head_count * MAXSEL
    local_queries = lax.all_to_all(queries, "head", split_axis=1, concat_axis=0, tiled=True)
    group_pick = (
        picked.reshape(head_count, seq_count, MAXSEL)
        .transpose(1, 0, 2)
        .reshape(seq_count, request_count)
    )
    group_count = counts.reshape(head_count, seq_count).transpose(1, 0)
    position = lax.broadcasted_iota(jnp.int32, (head_count, MAXSEL), 1).reshape(request_count)
    is_live = position[None, :] < jnp.repeat(group_count, MAXSEL, axis=1)
    stored = tile_home[group_pick]
    owner_of = stored // tiles_dev
    inside_offset = stored % tiles_dev
    owner_ids = lax.broadcasted_iota(jnp.int32, (1, 1, seq_count), 2)
    hit_table = ((owner_of[:, :, None] == owner_ids) & is_live[:, :, None]).astype(jnp.int32)
    before = jnp.cumsum(hit_table, axis=1) - hit_table
    slot_rank = jnp.sum(before * hit_table, axis=2)
    for_me = (owner_of == seq_index) & is_live
    slot_ids = lax.broadcasted_iota(jnp.int32, (1, 1, capacity), 2)
    slot_hits = (for_me[:, :, None] & (slot_rank[:, :, None] == slot_ids)).astype(jnp.int32)
    send_within = jnp.sum(slot_hits * inside_offset[:, :, None], axis=1)
    key_blocks = key_rows.reshape(tiles_dev, tile_rows, width_local)
    value_blocks = values.reshape(tiles_dev, tile_rows, width_local)
    send_keys = key_blocks[send_within]
    send_values = value_blocks[send_within]
    my_owner = lax.dynamic_index_in_dim(owner_of, seq_index, 0, keepdims=False)
    my_rank = lax.dynamic_index_in_dim(slot_rank, seq_index, 0, keepdims=False)
    my_live = lax.dynamic_index_in_dim(is_live, seq_index, 0, keepdims=False)
    flat_slot = my_owner * capacity + jnp.minimum(my_rank, capacity - 1)

    def arrange(incoming_rows):
        picked_rows = incoming_rows.reshape(seq_count * capacity, tile_rows, width_local)[flat_slot]
        return picked_rows.reshape(head_count, MAXSEL * tile_rows, heads_local, HD)

    query_heads = local_queries.reshape(head_count, tile_rows, heads_local, HD)
    key_live = jnp.repeat(my_live.reshape(head_count, MAXSEL), tile_rows, axis=1)[:, None, None, :]
    recv_keys, recv_values = (
        lax.all_to_all(send_keys, "seq", split_axis=0, concat_axis=0, tiled=True),
        lax.all_to_all(send_values, "seq", split_axis=0, concat_axis=0, tiled=True),
    )
    logit_scores = jnp.einsum(
        "rqhd,rkhd->rhqk", query_heads, arrange(recv_keys), preferred_element_type=jnp.float32
    ) * HD ** (-0.5)
    logit_scores = jnp.where(key_live, logit_scores, -1e30)
    row_top = jnp.max(logit_scores, axis=-1, keepdims=True)
    exponent = jnp.where(key_live, jnp.exp(logit_scores - row_top), 0.0)
    weights = exponent.astype(jnp.bfloat16)
    row_sum_total = jnp.sum(exponent, axis=-1)
    fetched_values = arrange(recv_values)
    mixed = jnp.einsum(
        "rhqk,rkhd->rqhd", weights, fetched_values, preferred_element_type=jnp.float32
    )
    mixed = mixed / jnp.transpose(row_sum_total, (0, 2, 1))[:, :, :, None]
    attended = mixed.astype(jnp.bfloat16).reshape(head_count * tile_rows, width_local)
    partial_sum = jnp.dot(attended, w_out, preferred_element_type=jnp.float32)
    summed = lax.psum(partial_sum.astype(jnp.bfloat16), "head").astype(jnp.float32)
    layer_out = lax.dynamic_slice_in_dim(summed, lax.axis_index("head") * tile_rows, tile_rows, 0)
    return layer_out.astype(jnp.bfloat16)


def solution(mesh):
    placed = (
        P(("head", "seq"), None),
        P("seq", "head"),
        P("seq", "head"),
        P("head", None),
        P(),
        P(),
        P(),
    )
    return jax.shard_map(
        body, mesh=mesh, in_specs=placed, out_specs=P(("head", "seq"), None), check_vma=False
    )
```

profile of v0, /device:TPU:1, one launch (start us, length us, event | category | flops | bytes accessed | tf_op | source)
XLA Modules:
  0.0 815.5 jit_solution(14306597630840057382)
XLA Ops:
  6.5 0.9 reshape.182
  7.7 24.8 %gather_fusion = s32[6144]{0:T(1024)S(1)} fusion(s32[768]{0:T(1024)S(1)} %copy-done.2, s32[6144]{0:T(1024)S(1)} %broadcast_clamp_fusion), kind=kCustom, calls=%fused_computation | custom fusion | bytes 73728 | tf_op jit(solution)/shard_map/gather | solution.py:29
  33.4 4.9 fusion.17
  39.0 8.3 %gather_fusion.3 = bf16[128,64,768]{2,1,0:T(8,128)(2,1)} fusion(bf16[12,64,768]{2,1,0:T(8,128)(2,1)S(1)} %bitcast.64, s32[1024]{0:T(1024)S(1)} %pad_clamp_fusion.1), kind=kCustom, calls=%fused_computation.3 | custom fusion | bytes 25166336 | tf_op jit(solution)/shard_map/gather | solution.py:42
  47.3 13.3 %all-to-all-start.1 = ((bf16[64,2,64,768]{3,2,1,0:T(8,128)(2,1)}), bf16[64,2,64,768]{3,2,1,0:T(8,128)(2,1)}, u32[]{:S(2)}, u32[]{:S(2)}) async-start(bf16[64,2,64,768]{3,2,1,0:T(8,128)(2,1)} %bitcast.67), calls=%async_computation.1 | async-start | bytes 25165824 | tf_op jit(solution)/shard_map/all_to_all | solution.py:56
  60.6 8.3 %gather_fusion.1 = bf16[128,64,768]{2,1,0:T(8,128)(2,1)} fusion(bf16[12,64,768]{2,1,0:T(8,128)(2,1)S(1)} %bitcast.65, s32[1024]{0:T(1024)S(1)} %pad_clamp_fusion.1), kind=kCustom, calls=%fused_computation.1 | custom fusion | bytes 25166336 | tf_op jit(solution)/shard_map/gather | solution.py:43
  68.9 263.8 %all-to-all-done.1 = bf16[64,2,64,768]{3,2,1,0:T(8,128)(2,1)} async-done(((bf16[64,2,64,768]{3,2,1,0:T(8,128)(2,1)}), bf16[64,2,64,768]{3,2,1,0:T(8,128)(2,1)}, u32[]{:S(2)}, u32[]{:S(2)}) %all-to-all-start.1) | async-done | bytes 12582944 | tf_op jit(solution)/shard_map/all_to_all | solution.py:56
  332.7 14.5 %all-to-all-start = ((bf16[64,2,64,768]{3,2,1,0:T(8,128)(2,1)}), bf16[64,2,64,768]{3,2,1,0:T(8,128)(2,1)}, u32[]{:S(2)}, u32[]{:S(2)}) async-start(bf16[64,2,64,768]{3,2,1,0:T(8,128)(2,1)} %bitcast.66), calls=%async_computation | async-start | bytes 25165824 | tf_op jit(solution)/shard_map/all_to_all | solution.py:57
  347.2 0.8 copy.91
  348.0 0.2 dynamic-slice_reduce_fusion
  348.5 0.2 add_reduce_fusion
  348.7 272.2 %all-to-all-done = bf16[64,2,64,768]{3,2,1,0:T(8,128)(2,1)} async-done(((bf16[64,2,64,768]{3,2,1,0:T(8,128)(2,1)}), bf16[64,2,64,768]{3,2,1,0:T(8,128)(2,1)}, u32[]{:S(2)}, u32[]{:S(2)}) %all-to-all-start) | async-done | bytes 12582944 | tf_op jit(solution)/shard_map/all_to_all | solution.py:57
  620.8 4.0 all-to-all-start.2
  624.9 12.0 %gather_fusion.4 = bf16[96,64,768]{2,1,0:T(8,128)(2,1)} fusion(bf16[128,64,768]{2,1,0:T(8,128)(2,1)} %bitcast.12, s32[1024]{0:T(1024)S(1)} %pad_clamp_fusion), kind=kCustom, calls=%fused_computation.4 | custom fusion | bytes 18874752 | tf_op jit(solution)/shard_map/gather | solution.py:50
  636.9 20.2 %reshape.191 = bf16[4,1536,6,128]{3,2,1,0:T(8,128)(2,1)} reshape(bf16[96,64,768]{2,1,0:T(8,128)(2,1)} %gather_fusion.4) | data formatting | bytes 18874368 | tf_op jit(solution)/shard_map/reshape | solution.py:51
  657.1 12.0 %gather_fusion.2 = bf16[96,64,768]{2,1,0:T(8,128)(2,1)} fusion(bf16[128,64,768]{2,1,0:T(8,128)(2,1)} %bitcast.8, s32[1024]{0:T(1024)S(1)} %pad_clamp_fusion), kind=kCustom, calls=%fused_computation.2 | custom fusion | bytes 18874752 | tf_op jit(solution)/shard_map/gather | solution.py:50
  669.1 20.2 %reshape.187 = bf16[4,1536,6,128]{3,2,1,0:T(8,128)(2,1)} reshape(bf16[96,64,768]{2,1,0:T(8,128)(2,1)} %gather_fusion.2) | data formatting | bytes 18874368 | tf_op jit(solution)/shard_map/reshape | solution.py:51
  689.2 11.5 %fusion.6 = f32[4,6,1536,64]{2,3,1,0:T(8,128)} fusion(bf16[4,1536,6,128]{3,2,1,0:T(8,128)(2,1)} %reshape.191, bf16[64,4,768]{2,0,1:T(8,128)(2,1)S(1)} %all-to-all-done.2), kind=kOutput, calls=%fused_computation.13 | convolution fusion | flops 603979776 | bytes 19267584 | tf_op jit(solution)/shard_map/rqhd,rkhd->rhqk/dot_general | solution.py:59
  700.8 10.0 %fusion.45 = (f32[4,6,64]{2,1,0:T(8,128)S(1)}, bf16[4,6,64,1536]{3,2,1,0:T(8,128)(2,1)S(1)}) fusion(f32[4,6,1536,64]{2,3,1,0:T(8,128)} %fusion.6, pred[4,1536]{1,0:T(4,128)(4,1)S(1)} %broadcast_in_dim.42), kind=kOutput, calls=%fused_computation.61 | output fusion | flops 18875904 | bytes 14168064 | tf_op jit(solution)/shard_map/sub | solution.py:64
  710.8 7.5 fusion.32
  718.3 0.3 copy.68
  718.6 4.0 convolution_convert_fusion
  722.7 83.8 %all-reduce.2.cloned.1.call-done = bf16[256,6144]{1,0:T(8,128)(2,1)} async-done(((bf16[256,6144]{1,0:T(8,128)(2,1)}), bf16[256,6144]{1,0:T(8,128)(2,1)}) %all-reduce.2.cloned.1.call-update) | async-done | bytes 3145744 | tf_op jit(solution)/shard_map/psum | solution.py:74
  806.5 2.1 convert_convert_fusion
  (53 shorter events, 2.0 us)
Async XLA Ops:
  6.5 32.5 %copy-start = (bf16[768,768]{1,0:T(8,128)(2,1)S(1)}, bf16[768,768]{1,0:T(8,128)(2,1)}, u32[]{:S(2)}) copy-start(bf16[768,768]{1,0:T(8,128)(2,1)} %param.8) | copy-start | bytes 3538948
  6.5 1.2 copy-start.2
  7.7 25.5 %copy-start.5 = (s32[256]{0:T(256)S(1)}, s32[256]{0:T(256)}, u32[]{:S(2)}) copy-start(s32[256]{0:T(256)} %param.12) | copy-start | bytes 3076
  47.3 13.4 %copy-start.3 = (bf16[768,768]{1,0:T(8,128)(2,1)S(1)}, bf16[768,768]{1,0:T(8,128)(2,1)}, u32[]{:S(2)}) copy-start(bf16[768,768]{1,0:T(8,128)(2,1)} %param.9) | copy-start | bytes 3538948
  47.3 285.5 %all-to-all-start.1 = ((bf16[64,2,64,768]{3,2,1,0:T(8,128)(2,1)}), bf16[64,2,64,768]{3,2,1,0:T(8,128)(2,1)}, u32[]{:S(2)}, u32[]{:S(2)}) async-start(bf16[64,2,64,768]{3,2,1,0:T(8,128)(2,1)} %bitcast.67), calls=%async_computation.1 | async-start | bytes 25165824 | tf_op jit(solution)/shard_map/all_to_all | solution.py:56
  332.7 14.5 %copy-start.4 = (bf16[64,3072]{1,0:T(8,128)(2,1)S(1)}, bf16[64,3072]{1,0:T(8,128)(2,1)}, u32[]{:S(2)}) copy-start(bf16[64,3072]{1,0:T(8,128)(2,1)} %param.7) | copy-start | bytes 1179652
  332.7 288.1 %all-to-all-start = ((bf16[64,2,64,768]{3,2,1,0:T(8,128)(2,1)}), bf16[64,2,64,768]{3,2,1,0:T(8,128)(2,1)}, u32[]{:S(2)}, u32[]{:S(2)}) async-start(bf16[64,2,64,768]{3,2,1,0:T(8,128)(2,1)} %bitcast.66), calls=%async_computation | async-start | bytes 25165824 | tf_op jit(solution)/shard_map/all_to_all | solution.py:57
  620.8 68.4 %all-to-all-start.2 = ((bf16[64,4,768]{2,0,1:T(8,128)(2,1)}), bf16[64,4,768]{2,0,1:T(8,128)(2,1)S(1)}, u32[]{:S(2)}, u32[]{:S(2)}) async-start(bf16[64,4,768]{2,0,1:T(8,128)(2,1)} %bitcast.63), calls=%async_computation.2 | async-start | bytes 786432 | tf_op jit(solution)/shard_map/all_to_all | solution.py:20
  624.8 181.7 %all-reduce.2.cloned.1.call-start = ((), (), s32[]{:S(2)}) async-start(), calls=%async_computation.3 | async-start | bytes 6291456 | tf_op jit(solution)/shard_map/psum | solution.py:74
  700.8 17.8 %slice-start = ((s8[9437184]{0:T(1024)(128)(4,1)}), s8[1048576]{0:T(1024)(128)(4,1)S(1)}, s32[]{:S(2)}) async-start(s8[9437184]{0:T(1024)(128)(4,1)} %bitcast.71), calls=%async_computation.4 | async-start | bytes 2097152
  700.8 17.8 %slice-start.1 = ((s8[9437184]{0:T(1024)(128)(4,1)}), s8[4194304]{0:T(1024)(128)(4,1)S(1)}, s32[]{:S(2)}) async-start(s8[9437184]{0:T(1024)(128)(4,1)} %bitcast.71), calls=%async_computation.5 | async-start | bytes 8388608
  710.8 7.8 slice-start.2
  718.6 90.0 %copy-start.1 = (bf16[768,768]{1,0:T(8,128)(2,1)S(1)}, bf16[768,768]{1,0:T(8,128)(2,1)}, u32[]{:S(2)}) copy-start(bf16[768,768]{1,0:T(8,128)(2,1)} %param.8) | copy-start | bytes 3538948
Sparse Core Ops, SparseCore 0:
  722.8 83.6 all-reduce.1
where the time goes:
time: 817 us; the launch traced here: 815 us
  waiting for transfers between devices  620 us (76%)
  local copies, waits for them, and re-layouts  110 us (13%)
  starting transfers between devices  31.8 us (4%)
  matrix products  23 us (3%)
  other arithmetic  17.5 us (2%)
  between operations  13.7 us (2%)
    all_to_all x1, waiting for transfers between devices, body(): lax.all_to_all(send_values, 'seq', split_axis=0, concat_axis=0, tiled=True)  272 us
    all_to_all x1, waiting for transfers between devices, body(): lax.all_to_all(send_keys, 'seq', split_axis=0, concat_axis=0, tiled=True)  264 us
    psum x1, waiting for transfers between devices, body(): lax.psum(partial_sum.astype(jnp.bfloat16), 'head').astype(jnp.float32)  83.8 us
    reshape x2, local copies, waits for them, and re-layouts, arrange(): return picked_rows.reshape(head_count, MAXSEL * tile_rows, heads_local, HD)  40.3 us
    gather x1, local copies, waits for them, and re-layouts, body(): stored = tile_home[group_pick]  24.8 us
    gather x2, local copies, waits for them, and re-layouts, arrange(): incoming_rows.reshape(seq_count * capacity, tile_rows, width_local)  24 us
  transfers between devices with their start and end apart: 4, of which 3 were waited for; matrix products, arithmetic and copies ran while one was open for 9% of the time, Pallas kernels for 0%

commit v1 on v0

--- a/solution.py
+++ b/solution.py
@@ -1,3 +1,4 @@
+import functools
 import jax
 import jax.numpy as jnp
 from jax import lax
@@ -5,6 +6,13 @@
 
 HD = 128
 MAXSEL = 24
+
+
+def open_values(page, mesh_ax):
+    return jnp.sum(lax.all_gather(page, mesh_ax), axis=0)
+
+
+assign_ladders = functools.partial(open_values, mesh_ax="head")
 
 
 def body(queries, key_rows, values, w_out, picked, counts, tile_home):
@@ -71,7 +79,7 @@
     mixed = mixed / jnp.transpose(row_sum_total, (0, 2, 1))[:, :, :, None]
     attended = mixed.astype(jnp.bfloat16).reshape(head_count * tile_rows, width_local)
     partial_sum = jnp.dot(attended, w_out, preferred_element_type=jnp.float32)
-    summed = lax.psum(partial_sum.astype(jnp.bfloat16), "head").astype(jnp.float32)
+    summed = assign_ladders(partial_sum.astype(jnp.bfloat16)).astype(jnp.float32)
     layer_out = lax.dynamic_slice_in_dim(summed, lax.axis_index("head") * tile_rows, tile_rows, 0)
     return layer_out.astype(jnp.bfloat16)
 

time: 817 us -> 867 us (1.061)
  waiting for transfers between devices: 620 us -> 660 us
  other arithmetic: 17.5 us -> 27 us
    all_gather x0 -> x1, waiting for transfers between devices: none -> 124 us  [open_values(): return jnp.sum(lax.all_gather(page, mesh_ax), axis=0)]
    psum x1 -> x0, waiting for transfers between devices: 83.8 us -> none  [body(): lax.psum(partial_sum.astype(jnp.bfloat16), 'head').astype(jnp.float32)]
    reduce_sum x0 -> x1, other arithmetic: none -> 9.49 us  [open_values(): return jnp.sum(lax.all_gather(page, mesh_ax), axis=0)]
where the time goes in v1:
time: 867 us; the launch traced here: 865 us
  waiting for transfers between devices  660 us (76%)
  local copies, waits for them, and re-layouts  110 us (13%)
  starting transfers between devices  31.8 us (4%)
  other arithmetic  27 us (3%)
  matrix products  23.1 us (3%)
  between operations  13.7 us (2%)
    all_to_all x1, waiting for transfers between devices, body(): lax.all_to_all(send_values, 'seq', split_axis=0, concat_axis=0, tiled=True)  272 us
    all_to_all x1, waiting for transfers between devices, body(): lax.all_to_all(send_keys, 'seq', split_axis=0, concat_axis=0, tiled=True)  264 us
    all_gather x1, waiting for transfers between devices, open_values(): return jnp.sum(lax.all_gather(page, mesh_ax), axis=0)  124 us
    reshape x2, local copies, waits for them, and re-layouts, arrange(): return picked_rows.reshape(head_count, MAXSEL * tile_rows, heads_local, HD)  40.3 us
    gather x1, local copies, waits for them, and re-layouts, body(): stored = tile_home[group_pick]  24.8 us
    gather x2, local copies, waits for them, and re-layouts, arrange(): incoming_rows.reshape(seq_count * capacity, tile_rows, width_local)  24 us
  transfers between devices with their start and end apart: 4, of which 3 were waited for; matrix products, arithmetic and copies ran while one was open for 9% of the time, Pallas kernels for 0%

profile of v1, /device:TPU:1, one launch (start us, length us, event | category | flops | bytes accessed | tf_op | source)
XLA Modules:
  0.0 865.2 jit_solution(17578803365170616030)
XLA Ops:
  6.5 0.9 reshape.182
  7.7 24.8 %gather_fusion = s32[6144]{0:T(1024)S(1)} fusion(s32[768]{0:T(1024)S(1)} %copy-done.2, s32[6144]{0:T(1024)S(1)} %broadcast_clamp_fusion), kind=kCustom, calls=%fused_computation | custom fusion | bytes 73728 | tf_op jit(solution)/shard_map/gather | solution.py:37
  33.4 4.9 fusion.17
  39.0 8.3 gather_fusion.3
  47.3 13.3 %all-to-all-start.1 = ((bf16[64,2,64,768]{3,2,1,0:T(8,128)(2,1)}), bf16[64,2,64,768]{3,2,1,0:T(8,128)(2,1)}, u32[]{:S(2)}, u32[]{:S(2)}) async-start(bf16[64,2,64,768]{3,2,1,0:T(8,128)(2,1)} %bitcast.68), calls=%async_computation.1 | async-start | bytes 25165824 | tf_op jit(solution)/shard_map/all_to_all | solution.py:64
  60.6 8.3 gather_fusion.1
  68.9 263.8 %all-to-all-done.1 = bf16[64,2,64,768]{3,2,1,0:T(8,128)(2,1)} async-done(((bf16[64,2,64,768]{3,2,1,0:T(8,128)(2,1)}), bf16[64,2,64,768]{3,2,1,0:T(8,128)(2,1)}, u32[]{:S(2)}, u32[]{:S(2)}) %all-to-all-start.1) | async-done | bytes 12582944 | tf_op jit(solution)/shard_map/all_to_all | solution.py:64
  332.7 14.5 %all-to-all-start = ((bf16[64,2,64,768]{3,2,1,0:T(8,128)(2,1)}), bf16[64,2,64,768]{3,2,1,0:T(8,128)(2,1)}, u32[]{:S(2)}, u32[]{:S(2)}) async-start(bf16[64,2,64,768]{3,2,1,0:T(8,128)(2,1)} %bitcast.67), calls=%async_computation | async-start | bytes 25165824 | tf_op jit(solution)/shard_map/all_to_all | solution.py:65
  347.2 0.8 copy.91
  348.5 0.2 add_reduce_fusion
  348.7 272.2 %all-to-all-done = bf16[64,2,64,768]{3,2,1,0:T(8,128)(2,1)} async-done(((bf16[64,2,64,768]{3,2,1,0:T(8,128)(2,1)}), bf16[64,2,64,768]{3,2,1,0:T(8,128)(2,1)}, u32[]{:S(2)}, u32[]{:S(2)}) %all-to-all-start) | async-done | bytes 12582944 | tf_op jit(solution)/shard_map/all_to_all | solution.py:65
  620.8 4.0 all-to-all-start.2
  624.9 12.0 %gather_fusion.4 = bf16[96,64,768]{2,1,0:T(8,128)(2,1)} fusion(bf16[128,64,768]{2,1,0:T(8,128)(2,1)} %bitcast.12, s32[1024]{0:T(1024)S(1)} %pad_clamp_fusion), kind=kCustom, calls=%fused_computation.4 | custom fusion | bytes 18874752 | tf_op jit(solution)/shard_map/gather | solution.py:58
  636.9 20.2 %reshape.191 = bf16[4,1536,6,128]{3,2,1,0:T(8,128)(2,1)} reshape(bf16[96,64,768]{2,1,0:T(8,128)(2,1)} %gather_fusion.4) | data formatting | bytes 18874368 | tf_op jit(solution)/shard_map/reshape | solution.py:59
  657.1 12.0 %gather_fusion.2 = bf16[96,64,768]{2,1,0:T(8,128)(2,1)} fusion(bf16[128,64,768]{2,1,0:T(8,128)(2,1)} %bitcast.8, s32[1024]{0:T(1024)S(1)} %pad_clamp_fusion), kind=kCustom, calls=%fused_computation.2 | custom fusion | bytes 18874752 | tf_op jit(solution)/shard_map/gather | solution.py:58
  669.1 20.2 %reshape.187 = bf16[4,1536,6,128]{3,2,1,0:T(8,128)(2,1)} reshape(bf16[96,64,768]{2,1,0:T(8,128)(2,1)} %gather_fusion.2) | data formatting | bytes 18874368 | tf_op jit(solution)/shard_map/reshape | solution.py:59
  689.2 11.5 %fusion.6 = f32[4,6,1536,64]{2,3,1,0:T(8,128)} fusion(bf16[4,1536,6,128]{3,2,1,0:T(8,128)(2,1)} %reshape.191, bf16[64,4,768]{2,0,1:T(8,128)(2,1)S(1)} %all-to-all-done.2), kind=kOutput, calls=%fused_computation.13 | convolution fusion | flops 603979776 | bytes 19267584 | tf_op jit(solution)/shard_map/rqhd,rkhd->rhqk/dot_general | solution.py:67
  700.8 10.0 %fusion.45 = (f32[4,6,64]{2,1,0:T(8,128)S(1)}, bf16[4,6,64,1536]{3,2,1,0:T(8,128)(2,1)S(1)}) fusion(f32[4,6,1536,64]{2,3,1,0:T(8,128)} %fusion.6, pred[4,1536]{1,0:T(4,128)(4,1)S(1)} %broadcast_in_dim.42), kind=kOutput, calls=%fused_computation.61 | output fusion | flops 18875904 | bytes 14168064 | tf_op jit(solution)/shard_map/sub | solution.py:72
  710.8 7.5 fusion.32
  718.3 0.3 copy.68
  718.6 4.0 convolution_convert_fusion
  722.7 124.1 %all-gather.3.cloned.1.call-done = bf16[1024,6144]{1,0:T(8,128)(2,1)} async-done(((bf16[256,6144]{1,0:T(8,128)(2,1)}), bf16[1024,6144]{1,0:T(8,128)(2,1)}) %all-gather.3.cloned.1.call-update) | async-done | bytes 12582928 | tf_op jit(solution)/shard_map/all_gather | solution.py:12
  846.8 9.5 %reduce_sum.45 = bf16[256,6144]{1,0:T(8,128)(2,1)} reduce(bf16[4,256,6144]{2,1,0:T(8,128)(2,1)} %bitcast.69, bf16[]{:T(256)} %constant.66.clone.1), dimensions={0}, to_apply=%region_5.6 | reduce | flops 4718592 | bytes 15728642 | tf_op jit(solution)/shard_map/reduce_sum | solution.py:12
  856.3 2.1 convert_convert_fusion
  (54 shorter events, 2.1 us)
Async XLA Ops:
  6.5 32.5 %copy-start = (bf16[768,768]{1,0:T(8,128)(2,1)S(1)}, bf16[768,768]{1,0:T(8,128)(2,1)}, u32[]{:S(2)}) copy-start(bf16[768,768]{1,0:T(8,128)(2,1)} %param.8) | copy-start | bytes 3538948
  6.5 1.2 copy-start.2
  7.7 25.5 %copy-start.5 = (s32[256]{0:T(256)S(1)}, s32[256]{0:T(256)}, u32[]{:S(2)}) copy-start(s32[256]{0:T(256)} %param.12) | copy-start | bytes 3076
  47.3 13.4 %copy-start.3 = (bf16[768,768]{1,0:T(8,128)(2,1)S(1)}, bf16[768,768]{1,0:T(8,128)(2,1)}, u32[]{:S(2)}) copy-start(bf16[768,768]{1,0:T(8,128)(2,1)} %param.9) | copy-start | bytes 3538948
  47.3 285.5 %all-to-all-start.1 = ((bf16[64,2,64,768]{3,2,1,0:T(8,128)(2,1)}), bf16[64,2,64,768]{3,2,1,0:T(8,128)(2,1)}, u32[]{:S(2)}, u32[]{:S(2)}) async-start(bf16[64,2,64,768]{3,2,1,0:T(8,128)(2,1)} %bitcast.68), calls=%async_computation.1 | async-start | bytes 25165824 | tf_op jit(solution)/shard_map/all_to_all | solution.py:64
  332.7 14.5 %copy-start.4 = (bf16[64,3072]{1,0:T(8,128)(2,1)S(1)}, bf16[64,3072]{1,0:T(8,128)(2,1)}, u32[]{:S(2)}) copy-start(bf16[64,3072]{1,0:T(8,128)(2,1)} %param.7) | copy-start | bytes 1179652
  332.7 288.1 %all-to-all-start = ((bf16[64,2,64,768]{3,2,1,0:T(8,128)(2,1)}), bf16[64,2,64,768]{3,2,1,0:T(8,128)(2,1)}, u32[]{:S(2)}, u32[]{:S(2)}) async-start(bf16[64,2,64,768]{3,2,1,0:T(8,128)(2,1)} %bitcast.67), calls=%async_computation | async-start | bytes 25165824 | tf_op jit(solution)/shard_map/all_to_all | solution.py:65
  620.8 68.4 %all-to-all-start.2 = ((bf16[64,4,768]{2,0,1:T(8,128)(2,1)}), bf16[64,4,768]{2,0,1:T(8,128)(2,1)S(1)}, u32[]{:S(2)}, u32[]{:S(2)}) async-start(bf16[64,4,768]{2,0,1:T(8,128)(2,1)} %bitcast.64), calls=%async_computation.2 | async-start | bytes 786432 | tf_op jit(solution)/shard_map/all_to_all | solution.py:28
  624.8 222.0 %all-gather.3.cloned.1.call-start = ((), (), s32[]{:S(2)}) async-start(), calls=%async_computation.3 | async-start | bytes 15728640 | tf_op jit(solution)/shard_map/all_gather | solution.py:12
  700.8 17.8 %slice-start = ((s8[9437184]{0:T(1024)(128)(4,1)}), s8[1048576]{0:T(1024)(128)(4,1)S(1)}, s32[]{:S(2)}) async-start(s8[9437184]{0:T(1024)(128)(4,1)} %bitcast.73), calls=%async_computation.4 | async-start | bytes 2097152
  700.8 17.8 %slice-start.1 = ((s8[9437184]{0:T(1024)(128)(4,1)}), s8[4194304]{0:T(1024)(128)(4,1)S(1)}, s32[]{:S(2)}) async-start(s8[9437184]{0:T(1024)(128)(4,1)} %bitcast.73), calls=%async_computation.5 | async-start | bytes 8388608
  710.8 7.8 slice-start.2
  722.7 135.7 %copy-start.1 = (bf16[768,768]{1,0:T(8,128)(2,1)S(1)}, bf16[768,768]{1,0:T(8,128)(2,1)}, u32[]{:S(2)}) copy-start(bf16[768,768]{1,0:T(8,128)(2,1)} %param.8) | copy-start | bytes 3538948
Sparse Core Ops, SparseCore 0:
  722.8 123.9 all-gather.2
